TPU v7x, 32 devices: a whole 2x2x4 slice. The times are simulated.
32 devices in a mesh: grp: 2 (over x), ctx: 16 (over z, y, core).
Axes of the slice: x: 2, y: 2, z: 4, core: 2. Of those that a mesh axis runs over, the one named last changes fastest.
Arguments:
- queries: bfloat16 [960, 4096], P(None, ('grp', 'ctx')), parts along dimension 1, may hold values from -6 to 6
- key_rows: bfloat16 [960, 4096], P(None, ('grp', 'ctx')), parts along dimension 1, may hold values from -6 to 6
- value_rows: bfloat16 [960, 4096], P(None, ('grp', 'ctx')), parts along dimension 1, may hold values from -6 to 6
- short_taps: float32 [3, 960, 7], replicated, may hold values from -2 to 2
- long_filter: bfloat16 [960, 2048], P('ctx'), may hold values from -0.125 to 0.125
Outputs:
- mixed: bfloat16 [960, 4096], P(None, ('grp', 'ctx')), parts along dimension 1
There are 2 independent parts, one for each index of `grp`. A program takes and returns all parts, laid end to end along the dimension named above; an argument that names none is the same for every part. Nothing has to cross between parts.
All inputs are finite; a program needn't handle non-finite values.
Results may differ from a plain program's by a relative error of at most 0.0057.
Values may be sent and summed in bfloat16 or wider, within the bound.
A program may use at most 64 MiB of HBM per device.

v0:
```python
import math
import jax
import jax.numpy as jnp
from jax import lax
from jax.sharding import PartitionSpec as P

TAPS = 7
precise = lax.Precision.HIGH


def with_halo(value, sides, width):
    for axis, dim in sides:
        size, length = (lax.axis_size(axis), value.shape[dim])
        up = [(i, (i + 1) % size) for i in range(size - 1)]
        down = [(j, i) for i, j in up]
        last = lax.slice_in_dim(value, length - width, length, axis=dim)
        leading = lax.slice_in_dim(value, 0, width, axis=dim)
        before = lax.ppermute(last, axis, up)
        after = lax.ppermute(leading, axis, down)
        value = jnp.concatenate([before, value, after], axis=dim)
    return value


def angles(count_rows, count_cols, modulus):
    row_ids = lax.broadcasted_iota(jnp.int32, (count_rows, count_cols), 0)
    col_ids = lax.broadcasted_iota(jnp.int32, (count_rows, count_cols), 1)
    phase = (row_ids * col_ids % modulus).astype(jnp.float32) * (2.0 * math.pi / modulus)
    return (jnp.cos(phase), jnp.sin(phase))


def fourier_tables(length):
    inner_len = min(128, length)
    padded_len = 2 * length
    outer_len = padded_len // inner_len
    cos_outer, sin_outer = angles(outer_len // 2, outer_len, outer_len)
    cos_twist, sin_twist = angles(outer_len, inner_len, padded_len)
    cos_inner, sin_inner = angles(inner_len, inner_len, inner_len)
    outer_fwd = jnp.stack([cos_outer, -sin_outer])
    inner_fwd = jnp.stack([jnp.stack([cos_inner, -sin_inner]), jnp.stack([sin_inner, cos_inner])])
    inner_inv = jnp.stack([jnp.stack([cos_inner, sin_inner]), jnp.stack([-sin_inner, cos_inner])])
    return (outer_fwd, cos_twist, sin_twist, inner_fwd, inner_inv, padded_len)


def forward(signal, tables):
    outer_fwd, cos_twist, sin_twist, inner_fwd, inner_inv, padded_len = tables
    shaped = signal.reshape(signal.shape[:-1] + (outer_fwd.shape[1], inner_fwd.shape[2]))
    first = jnp.einsum("...ab,caf->...cfb", shaped, outer_fwd, precision=precise)
    first_real = first[..., 0, :, :]
    first_imag = first[..., 1, :, :]
    twist = jnp.stack(
        [
            first_real * cos_twist + first_imag * sin_twist,
            first_imag * cos_twist - first_real * sin_twist,
        ],
        axis=-3,
    )
    return jnp.einsum("...cfb,cdbk->...dfk", twist, inner_fwd, precision=precise)


def inverse(spectrum, tables):
    outer_fwd, cos_twist, sin_twist, inner_fwd, inner_inv, padded_len = tables
    first = jnp.einsum("...cfk,cdkb->...dfb", spectrum, inner_inv, precision=precise)
    first_real = first[..., 0, :, :]
    first_imag = first[..., 1, :, :]
    twist = jnp.stack(
        [
            first_real * cos_twist - first_imag * sin_twist,
            first_imag * cos_twist + first_real * sin_twist,
        ],
        axis=-3,
    )
    result = jnp.einsum("...cfb,caf->...ab", twist, outer_fwd, precision=precise)
    result = result / padded_len
    return result.reshape(result.shape[:-2] + (result.shape[-2] * result.shape[-1],))


def on_device(queries, key_rows, value_rows, short_taps, long_filter):
    tokens = queries.shape[1]
    rim_width = TAPS - 1
    stacked = jnp.stack([queries, key_rows, value_rows])
    padded = with_halo(stacked, (("ctx", 2),), rim_width)
    mirrored_taps = short_taps[:, ::-1, :]
    causal = jnp.zeros(stacked.shape, jnp.float32)
    anticausal = jnp.zeros(stacked.shape, jnp.float32)
    for offset in range(TAPS):
        begin = rim_width - offset
        causal = causal + short_taps[:, :, offset, None] * padded[:, :, begin : begin + tokens]
        later = rim_width + offset
        anticausal = (
            anticausal + mirrored_taps[:, :, offset, None] * padded[:, :, later : later + tokens]
        )
    product_a = (causal[1] * causal[2]).astype(jnp.bfloat16)
    product_b = (anticausal[1] * anticausal[2]).astype(jnp.bfloat16)
    tables = fourier_tables(long_filter.shape[1])
    outgoing = jnp.stack([product_a, product_b[::-1]])
    channel_rows = lax.all_to_all(outgoing, "ctx", split_axis=1, concat_axis=2, tiled=True)
    filter_spec = forward(long_filter.astype(jnp.float32), tables)
    data_spec = forward(channel_rows.astype(jnp.float32), tables)
    filter_real = filter_spec[:, 0]
    filter_imag = filter_spec[:, 1]
    data_real = data_spec[:, :, 0]
    data_imag = data_spec[:, :, 1]
    first_real = filter_real * data_real[0] - filter_imag * data_imag[0]
    first_imag = filter_real * data_imag[0] + filter_imag * data_real[0]
    second_real = filter_real * data_real[1] + filter_imag * data_imag[1]
    second_imag = filter_real * data_imag[1] - filter_imag * data_real[1]
    spectrum = jnp.stack(
        [jnp.stack([first_real, first_imag], axis=1), jnp.stack([second_real, second_imag], axis=1)]
    )
    convolved = inverse(spectrum, tables).astype(jnp.bfloat16)
    token_rows = lax.all_to_all(convolved, "ctx", split_axis=2, concat_axis=1, tiled=True)
    mixed_b = token_rows[1][::-1]
    result = causal[0] * token_rows[0].astype(jnp.float32) + anticausal[0] * mixed_b.astype(
        jnp.float32
    )
    return result.astype(jnp.bfloat16)


def solution(mesh):
    placed = (
        P(None, ("grp", "ctx")),
        P(None, ("grp", "ctx")),
        P(None, ("grp", "ctx")),
        P(),
        P("ctx", None),
    )
    return jax.shard_map(
        on_device, mesh=mesh, in_specs=placed, out_specs=P(None, ("grp", "ctx")), check_vma=False
    )
```

profile of v0, /device:TPU:0, one launch (start us, length us, event | category | flops | bytes accessed | tf_op | source)
XLA Modules:
  0.0 102.4 jit_solution(13261690223920789769)
XLA Ops:
  0.0 1.3 %pad_maximum_fusion.2 = bf16[3,960,128]{2,1,0:T(8,128)(2,1)S(1)} fusion(bf16[1,960,128]{2,1,0:T(8,128)(2,1)} %bitcast.184, bf16[1,960,128]{2,1,0:T(8,128)(2,1)} %bitcast.188, bf16[1,960,128]{2,1,0:T(8,128)(2,1)} %bitcast.192), kind=kLoop, calls=%fused_computation.55 | loop fusion | flops 737280 | bytes 1474560 | tf_op jit(solution)/shard_map/stack | solution.py:80
  1.9 1.3 %collective-permute-start.1 = (bf16[3,960,6]{1,2,0:T(8,128)(2,1)S(1)}, bf16[3,960,6]{1,2,0:T(8,128)(2,1)S(1)}, u32[]{:S(2)}, u32[]{:S(2)}) collective-permute-start(bf16[3,960,6]{1,2,0:T(8,128)(2,1)S(1)} %copy.51), channel_id=1, source_target_pairs={{1,0},{2,1},{3,2},{4,3},{5,4},{6,5},{7,6},{8,7},{9,8},{10,9},{11,1... | collective-permute-start | bytes 103688 | tf_op jit(solution)/shard_map/ppermute | solution.py:19
  3.5 3.0 %collective-permute-start = (bf16[3,960,6]{1,2,0:T(8,128)(2,1)S(1)}, bf16[3,960,6]{1,2,0:T(8,128)(2,1)S(1)}, u32[]{:S(2)}, u32[]{:S(2)}) collective-permute-start(bf16[3,960,6]{1,2,0:T(8,128)(2,1)S(1)} %copy.47), channel_id=1, source_target_pairs={{0,1},{1,2},{2,3},{3,4},{4,5},{5,6},{6,7},{7,8},{8,9},{9,10},{10,1... | collective-permute-start | bytes 103688 | tf_op jit(solution)/shard_map/ppermute | solution.py:18
  7.3 0.7 reverse.8
  8.1 0.7 reverse.7
  9.0 0.7 reverse.12
  10.4 0.7 reverse.11
  11.2 0.7 reverse.10
  15.4 0.7 fusion.60
  16.7 0.7 reverse.13
  18.7 1.2 %copy.52 = bf16[3,960,6]{2,1,0:T(8,128)(2,1)} copy(bf16[3,960,6]{1,2,0:T(8,128)(2,1)S(1)} %collective-permute-done.1) | data formatting | bytes 69120 | tf_op jit(solution)/shard_map/ppermute | solution.py:19
  19.9 2.5 %maximum_maximum_fusion = (bf16[3,960,134]{2,1,0:T(8,128)(2,1)S(1)}, bf16[3,960,134]{2,1,0:T(8,128)(2,1)S(1)}) fusion(bf16[1,960,128]{2,1,0:T(8,128)(2,1)S(1)} %bitcast.185, bf16[1,960,128]{2,1,0:T(8,128)(2,1)S(1)} %bitcast.189, bf16[1,960,128]{2,1,0:T(8,128)(2,1)S(1)} %bitcast.193, bf16[3,960,6]{2,1,0:T(8,128)(2,1)S(1)} %copy.48, bf16[3,960,6]{2,1,0:T(8,128)(2,1)} %copy.52), kind=kLoop, calls=%fused_computation.39 | loop fusion | flops 6174720 | bytes 2350080 | tf_op jit(solution)/shard_map/concatenate | solution.py:20
  22.6 4.5 %fusion.31 = f32[3,960,128]{2,1,0:T(8,128)S(1)} fusion(bf16[3,960,134]{2,1,0:T(8,128)(2,1)S(1)} %get-tuple-element.16, f32[3,960]{1,0:T(4,128)S(1)} %copy-done.13, f32[3,960]{1,0:T(4,128)S(1)} %copy-done.14, f32[3,960]{1,0:T(4,128)S(1)} %copy-done.17, f32[3,960]{1,0:T(4,128)S(1)} %copy-done.18, f32[3,960]{1,0:T(4,128)S(1)} %copy-done.15, ...), kind=kLoop, calls=%fused_computation.38 | loop fusion | flops 8110080 | bytes 6716160 | tf_op jit(solution)/shard_map/add | solution.py:90
  27.1 1.1 %copy-done = f32[3,960,128]{2,1,0:T(8,128)} copy-done((f32[3,960,128]{2,1,0:T(8,128)}, f32[3,960,128]{2,1,0:T(8,128)S(1)}, u32[]{:S(2)}) %copy-start) | copy-done | bytes 1474584
  29.0 4.3 %fusion.25 = f32[3,960,128]{2,1,0:T(8,128)S(1)} fusion(bf16[3,960,134]{2,1,0:T(8,128)(2,1)S(1)} %get-tuple-element.15, f32[3,960]{1,0:T(4,128)S(1)} %get-tuple-element.34, f32[3,960]{1,0:T(4,128)S(1)} %get-tuple-element.35, f32[3,960]{1,0:T(4,128)S(1)} %copy-done.11, f32[3,960]{1,0:T(4,128)S(1)} %copy-done.12, f32[3,960]{1,0:T(4,128)S(1)} %copy-done.9, ...), kind=kLoop, calls=%fused_computation.32 | loop fusion | flops 8110080 | bytes 6716160 | tf_op jit(solution)/shard_map/add | solution.py:87
  33.3 1.1 %copy-done.1 = f32[3,960,128]{2,1,0:T(8,128)} copy-done((f32[3,960,128]{2,1,0:T(8,128)}, f32[3,960,128]{2,1,0:T(8,128)S(1)}, u32[]{:S(2)}) %copy-start.1) | copy-done | bytes 1474584
  34.5 1.3 %copy.53 = bf16[2,960,128]{2,0,1:T(2,128)(2,1)} copy(bf16[2,960,128]{2,1,0:T(8,128)(2,1)S(1)} %pad_maximum_fusion.3) | data formatting | bytes 983040 | tf_op jit(solution)/shard_map/stack | solution.py:95
  35.8 8.1 %all-to-all-start = ((bf16[2,960,128]{2,0,1:T(2,128)(2,1)}), bf16[2,960,128]{2,0,1:T(2,128)(2,1)S(1)}, u32[]{:S(2)}, u32[]{:S(2)}) async-start(bf16[2,960,128]{2,0,1:T(2,128)(2,1)} %copy.53), calls=%async_computation | async-start | bytes 983040 | tf_op jit(solution)/shard_map/all_to_all | solution.py:96
  45.2 2.0 %fusion.17 = f32[60,2,32,128]{3,0,2,1:T(8,128)S(1)} fusion(f32[60,2,32,128]{3,2,0,1:T(8,128)S(1)} %pad_maximum_fusion, f32[1,2,128,128]{3,2,0,1:T(8,128)S(1)} %get-tuple-element.22, f32[1,2,128,128]{3,2,0,1:T(8,128)S(1)} %get-tuple-element.32), kind=kOutput, calls=%fused_computation.25 | convolution fusion | flops 755040256 | bytes 4194304 | tf_op jit(solution)/shard_map/...cfb,cdbk->...dfk/dot_general | solution.py:57
  47.2 10.4 %all-to-all-done = bf16[2,960,128]{2,0,1:T(2,128)(2,1)S(1)} async-done(((bf16[2,960,128]{2,0,1:T(2,128)(2,1)}), bf16[2,960,128]{2,0,1:T(2,128)(2,1)S(1)}, u32[]{:S(2)}, u32[]{:S(2)}) %all-to-all-start) | async-done | bytes 491552 | tf_op jit(solution)/shard_map/all_to_all | solution.py:96
  57.6 1.2 %convolution_bitcast_fusion = f32[2,60,2,32,128]{4,3,1,0,2:T(8,128)S(1)} fusion(bf16[2,16,60,128]{3,0,2,1:T(2,128)(2,1)S(1)} %bitcast.196, f32[1,16,32]{2,1,0:T(8,128)S(1)} %get-tuple-element.46, f32[1,16,32]{2,1,0:T(8,128)S(1)} %get-tuple-element.47), kind=kOutput, calls=%fused_computation.17 | convolution fusion | flops 94372864 | bytes 4427776 | tf_op jit(solution)/shard_map/...ab,caf->...cfb/dot_general | solution.py:47
  58.8 0.8 multiply_add_fusion.1
  60.0 5.0 %fusion.8 = f32[2,60,2,32,128]{4,1,3,2,0:T(8,128)S(1)} fusion(f32[2,60,2,32,128,1]{4,3,1,0,2,5:T(8,128)S(1)} %maximum_bitcast_fusion.1, f32[1,2,128,128]{3,2,0,1:T(8,128)S(1)} %get-tuple-element.22, f32[1,2,128,128]{3,2,0,1:T(8,128)S(1)} %get-tuple-element.32), kind=kOutput, calls=%fused_computation.10 | convolution fusion | flops 1510014976 | bytes 8126464 | tf_op jit(solution)/shard_map/...cfb,cdbk->...dfk/dot_general | solution.py:57
  65.0 1.0 multiply_subtract_fusion.3
  67.3 4.5 %fusion.14 = f32[2,60,2,32,128]{4,3,1,0,2:T(8,128)S(1)} fusion(f32[2,60,2,32,128,1]{4,1,3,2,0,5:T(8,128)S(1)} %maximum_bitcast_fusion, f32[1,2,128,128]{3,2,1,0:T(8,128)S(1)} %copy-done.7, f32[1,2,128,128]{3,2,1,0:T(8,128)S(1)} %copy-done.6), kind=kOutput, calls=%fused_computation.16 | convolution fusion | flops 1510014976 | bytes 8126464 | tf_op jit(solution)/shard_map/...cfk,cdkb->...dfb/dot_general | solution.py:62
  72.4 1.3 %fusion.41 = bf16[2,60,16,128]{3,2,1,0:T(8,128)(2,1)S(1)} fusion(f32[2,60,1,32,128]{4,3,1,0,2:T(8,128)S(1)} %get-tuple-element.10, f32[2,60,1,32,128]{4,3,1,0,2:T(8,128)S(1)} %get-tuple-element.9, f32[1,16,32]{2,1,0:T(8,128)S(1)} %get-tuple-element.46, f32[1,16,32]{2,1,0:T(8,128)S(1)} %get-tuple-element.47), kind=kOutput, calls=%fused_computation.44 | convolution fusion | flops 95847424 | bytes 4427776 | tf_op jit(solution)/shard_map/...cfb,caf->...ab/dot_general | solution.py:72
  73.7 0.8 copy.89
  74.6 2.8 %reshape.225 = bf16[16,2,7680]{2,1,0:T(2,128)(2,1)S(1)} reshape(bf16[2048,2,60]{2,1,0:T(2,128)(2,1)S(1)} %bitcast.182) | data formatting | bytes 983040
  77.4 17.7 %all_to_all.30 = bf16[16,2,7680]{2,1,0:T(2,128)(2,1)S(1)} all-to-all(bf16[16,2,7680]{2,1,0:T(2,128)(2,1)S(1)} %reshape.225), channel_id=1, replica_groups=mesh['grp'=2,'ctx'=16] {'ctx'}, dimensions={0} | all-to-all | bytes 983040 | tf_op jit(solution)/shard_map/all_to_all | solution.py:111
  95.0 3.5 %reshape.226 = bf16[2048,2,60]{2,1,0:T(2,128)(2,1)S(1)} reshape(bf16[16,2,7680]{2,1,0:T(2,128)(2,1)S(1)} %all_to_all.30) | data formatting | bytes 983040
  98.6 0.8 copy.88
  100.4 2.0 %fusion.46 = bf16[960,128]{1,0:T(8,128)(2,1)} fusion(f32[3,960,128]{2,1,0:T(8,128)} %copy-done, f32[960,128]{1,0:T(8,128)S(1)} %reshape.208, f32[3,960,128]{2,1,0:T(8,128)} %copy-done.1, bf16[960,128]{1,0:T(8,128)(2,1)S(1)} %rev.8), kind=kLoop, calls=%fused_computation.59 | loop fusion | flops 614400 | bytes 1966080 | tf_op jit(solution)/shard_map/convert_element_type | solution.py:116
  (86 shorter events, 13.1 us)
Async XLA Ops:
  1.3 5.9 %copy-start.8 = (f32[3,960,7]{1,2,0:T(8,128)S(1)}, f32[3,960,7]{1,2,0:T(8,128)}, u32[]{:S(2)}) copy-start(f32[3,960,7]{1,2,0:T(8,128)} %param.8) | copy-start | bytes 241924
  1.6 16.6 %copy-start.5 = (bf16[60,2048]{1,0:T(8,128)(2,1)S(1)}, bf16[60,2048]{1,0:T(8,128)(2,1)}, u32[]{:S(2)}) copy-start(bf16[60,2048]{1,0:T(8,128)(2,1)} %param.9) | copy-start | bytes 737284
  1.9 16.8 %collective-permute-start.1 = (bf16[3,960,6]{1,2,0:T(8,128)(2,1)S(1)}, bf16[3,960,6]{1,2,0:T(8,128)(2,1)S(1)}, u32[]{:S(2)}, u32[]{:S(2)}) collective-permute-start(bf16[3,960,6]{1,2,0:T(8,128)(2,1)S(1)} %copy.51), channel_id=1, source_target_pairs={{1,0},{2,1},{3,2},{4,3},{5,4},{6,5},{7,6},{8,7},{9,8},{10,9},{11,1... | collective-permute-start | bytes 103688 | tf_op jit(solution)/shard_map/ppermute | solution.py:19
  3.5 14.7 %collective-permute-start = (bf16[3,960,6]{1,2,0:T(8,128)(2,1)S(1)}, bf16[3,960,6]{1,2,0:T(8,128)(2,1)S(1)}, u32[]{:S(2)}, u32[]{:S(2)}) collective-permute-start(bf16[3,960,6]{1,2,0:T(8,128)(2,1)S(1)} %copy.47), channel_id=1, source_target_pairs={{0,1},{1,2},{2,3},{3,4},{4,5},{5,6},{6,7},{7,8},{8,9},{9,10},{10,1... | collective-permute-start | bytes 103688 | tf_op jit(solution)/shard_map/ppermute | solution.py:18
  6.9 13.0 %copy-start.2 = (bf16[960,128]{1,0:T(8,128)(2,1)S(1)}, bf16[960,128]{1,0:T(8,128)(2,1)}, u32[]{:S(2)}) copy-start(bf16[960,128]{1,0:T(8,128)(2,1)} %param.7) | copy-start | bytes 737284
  6.9 13.0 %copy-start.3 = (bf16[960,128]{1,0:T(8,128)(2,1)S(1)}, bf16[960,128]{1,0:T(8,128)(2,1)}, u32[]{:S(2)}) copy-start(bf16[960,128]{1,0:T(8,128)(2,1)} %param.6) | copy-start | bytes 737284
  6.9 13.0 %copy-start.4 = (bf16[960,128]{1,0:T(8,128)(2,1)S(1)}, bf16[960,128]{1,0:T(8,128)(2,1)}, u32[]{:S(2)}) copy-start(bf16[960,128]{1,0:T(8,128)(2,1)} %param.5) | copy-start | bytes 737284
  19.9 2.6 %copy-start.13 = (f32[3,960]{1,0:T(4,128)S(1)}, f32[3,960]{1,0:T(4,128)}, u32[]{:S(2)}) copy-start(f32[3,960]{1,0:T(4,128)} %get-tuple-element.40) | copy-start | bytes 34564
  19.9 2.6 %copy-start.14 = (f32[3,960]{1,0:T(4,128)S(1)}, f32[3,960]{1,0:T(4,128)}, u32[]{:S(2)}) copy-start(f32[3,960]{1,0:T(4,128)} %get-tuple-element.41) | copy-start | bytes 34564
  19.9 2.6 %copy-start.15 = (f32[3,960]{1,0:T(4,128)S(1)}, f32[3,960]{1,0:T(4,128)}, u32[]{:S(2)}) copy-start(f32[3,960]{1,0:T(4,128)} %get-tuple-element.44) | copy-start | bytes 34564
  19.9 2.6 %copy-start.16 = (f32[3,960]{1,0:T(4,128)S(1)}, f32[3,960]{1,0:T(4,128)}, u32[]{:S(2)}) copy-start(f32[3,960]{1,0:T(4,128)} %get-tuple-element.45) | copy-start | bytes 34564
  19.9 2.6 %copy-start.17 = (f32[3,960]{1,0:T(4,128)S(1)}, f32[3,960]{1,0:T(4,128)}, u32[]{:S(2)}) copy-start(f32[3,960]{1,0:T(4,128)} %get-tuple-element.42) | copy-start | bytes 34564
  19.9 2.6 %copy-start.18 = (f32[3,960]{1,0:T(4,128)S(1)}, f32[3,960]{1,0:T(4,128)}, u32[]{:S(2)}) copy-start(f32[3,960]{1,0:T(4,128)} %get-tuple-element.43) | copy-start | bytes 34564
  19.9 2.6 %copy-start.20 = (f32[3,960,1]{1,0,2:T(4,128)S(1)}, f32[3,960,1]{1,0,2:T(4,128)}, u32[]{:S(2)}) copy-start(f32[3,960,1]{1,0,2:T(4,128)} %copy.139) | copy-start | bytes 34564
  22.5 6.4 %copy-start.9 = (f32[3,960]{1,0:T(4,128)S(1)}, f32[3,960]{1,0:T(4,128)}, u32[]{:S(2)}) copy-start(f32[3,960]{1,0:T(4,128)} %get-tuple-element.38) | copy-start | bytes 34564
  22.5 6.4 %copy-start.10 = (f32[3,960]{1,0:T(4,128)S(1)}, f32[3,960]{1,0:T(4,128)}, u32[]{:S(2)}) copy-start(f32[3,960]{1,0:T(4,128)} %get-tuple-element.39) | copy-start | bytes 34564
  22.6 6.4 %copy-start.11 = (f32[3,960]{1,0:T(4,128)S(1)}, f32[3,960]{1,0:T(4,128)}, u32[]{:S(2)}) copy-start(f32[3,960]{1,0:T(4,128)} %get-tuple-element.36) | copy-start | bytes 34564
  22.6 6.4 %copy-start.12 = (f32[3,960]{1,0:T(4,128)S(1)}, f32[3,960]{1,0:T(4,128)}, u32[]{:S(2)}) copy-start(f32[3,960]{1,0:T(4,128)} %get-tuple-element.37) | copy-start | bytes 34564
  22.6 6.4 %copy-start.19 = (f32[3,960,1]{1,0,2:T(4,128)S(1)}, f32[3,960,1]{1,0,2:T(4,128)}, u32[]{:S(2)}) copy-start(f32[3,960,1]{1,0,2:T(4,128)} %copy.140) | copy-start | bytes 34564
  27.1 1.1 %copy-start = (f32[3,960,128]{2,1,0:T(8,128)}, f32[3,960,128]{2,1,0:T(8,128)S(1)}, u32[]{:S(2)}) copy-start(f32[3,960,128]{2,1,0:T(8,128)S(1)} %fusion.31) | copy-start | bytes 4423684
  33.3 1.1 %copy-start.1 = (f32[3,960,128]{2,1,0:T(8,128)}, f32[3,960,128]{2,1,0:T(8,128)S(1)}, u32[]{:S(2)}) copy-start(f32[3,960,128]{2,1,0:T(8,128)S(1)} %fusion.25) | copy-start | bytes 4423684
  35.8 21.7 %all-to-all-start = ((bf16[2,960,128]{2,0,1:T(2,128)(2,1)}), bf16[2,960,128]{2,0,1:T(2,128)(2,1)S(1)}, u32[]{:S(2)}, u32[]{:S(2)}) async-start(bf16[2,960,128]{2,0,1:T(2,128)(2,1)} %copy.53), calls=%async_computation | async-start | bytes 983040 | tf_op jit(solution)/shard_map/all_to_all | solution.py:96
  66.3 0.9 copy-start.6
  66.4 1.0 copy-start.7
where the time goes:
time: 103 us; the launch traced here: 102 us
  local copies, waits for them, and re-layouts  26.3 us (26%)
  other arithmetic  20.2 us (20%)
  blocking collectives  17.7 us (17%)
  matrix products  14.7 us (14%)
  starting transfers between devices  12.5 us (12%)
  waiting for transfers between devices  10.4 us (10%)
    unnamed x67, local copies, waits for them, and re-layouts  19.2 us
    all_to_all x1, blocking collectives, on_device(): lax.all_to_all(convolved, 'ctx', split_axis=2, concat_axis=1, tiled=True)  17.7 us
    all_to_all x1, waiting for transfers between devices, on_device(): lax.all_to_all(outgoing, 'ctx', split_axis=1, concat_axis=2, tiled=True)  10.4 us
    all_to_all x1, starting transfers between devices, on_device(): lax.all_to_all(outgoing, 'ctx', split_axis=1, concat_axis=2, tiled=True)  8.13 us
    dot_general x2, matrix products, forward(): jnp.einsum('...cfb,cdbk->...dfk', twist, inner_fwd, precision=precise)  6.97 us
    add x1, other arithmetic, on_device(): anticausal + mirrored_taps[:, :, offset, None] * padded[:, :, later:later...  4.54 us
    dot_general x1, matrix products, inverse(): jnp.einsum('...cfk,cdkb->...dfb', spectrum, inner_inv, precision=precise)  4.47 us
    add x1, other arithmetic, on_device(): causal + short_taps[:, :, offset, None] * padded[:, :, begin:begin + tokens]  4.31 us
  transfers between devices with their start and end apart: 3, of which 1 were waited for; matrix products, arithmetic and copies ran while one was open for 15% of the time, Pallas kernels for 0%

commit v1 on v0

--- a/solution.py
+++ b/solution.py
@@ -6,6 +6,13 @@
 
 TAPS = 7
 precise = lax.Precision.HIGH
+
+
+def exchange_blocks(block, name, split, join):
+    n_dev = lax.axis_size(name)
+    blocks = jnp.stack(jnp.split(block, n_dev, axis=split), axis=0)
+    blocks = lax.all_to_all(blocks, name, split_axis=0, concat_axis=0)
+    return jnp.concatenate(blocks, axis=join)
 
 
 def with_halo(value, sides, width):
@@ -108,7 +115,7 @@
         [jnp.stack([first_real, first_imag], axis=1), jnp.stack([second_real, second_imag], axis=1)]
     )
     convolved = inverse(spectrum, tables).astype(jnp.bfloat16)
-    token_rows = lax.all_to_all(convolved, "ctx", split_axis=2, concat_axis=1, tiled=True)
+    token_rows = exchange_blocks(convolved, "ctx", 2, 1)
     mixed_b = token_rows[1][::-1]
     result = causal[0] * token_rows[0].astype(jnp.float32) + anticausal[0] * mixed_b.astype(
         jnp.float32

time: 103 us -> 97.2 us (0.944)
  local copies, waits for them, and re-layouts: 26.3 us -> 19.1 us
  other arithmetic: 20.2 us -> 21.8 us
    unnamed x67 -> x80, local copies, waits for them, and re-layouts: 19.2 us -> 13.5 us
    slice x1, other arithmetic: 0.07 us -> 1.66 us  [on_device(): mixed_b = token_rows[1][::-1]]
  transfers between devices with their start and end apart: 3 -> 3, of which waited for: 1 -> 1; matrix products, arithmetic and copies ran while one was open for 15% -> 16% of each run, Pallas kernels for 0% -> 0%
where the time goes in v1:
time: 97.2 us; the launch traced here: 96.8 us
  other arithmetic  21.8 us (22%)
  local copies, waits for them, and re-layouts  19.1 us (20%)
  blocking collectives  17.7 us (18%)
  matrix products  14.7 us (15%)
  starting transfers between devices  12.5 us (13%)
  waiting for transfers between devices  10.4 us (11%)
    all_to_all x1, blocking collectives, exchange_blocks(): blocks = lax.all_to_all(blocks, name, split_axis=0, concat_axis=0)  17.7 us
    unnamed x80, local copies, waits for them, and re-layouts  13.5 us
    all_to_all x1, waiting for transfers between devices, on_device(): lax.all_to_all(outgoing, 'ctx', split_axis=1, concat_axis=2, tiled=True)  10.4 us
    all_to_all x1, starting transfers between devices, on_device(): lax.all_to_all(outgoing, 'ctx', split_axis=1, concat_axis=2, tiled=True)  8.13 us
    dot_general x2, matrix products, forward(): jnp.einsum('...cfb,cdbk->...dfk', twist, inner_fwd, precision=precise)  6.97 us
    add x1, other arithmetic, on_device(): anticausal + mirrored_taps[:, :, offset, None] * padded[:, :, later:later...  4.54 us
    dot_general x1, matrix products, inverse(): jnp.einsum('...cfk,cdkb->...dfb', spectrum, inner_inv, precision=precise)  4.47 us
    add x1, other arithmetic, on_device(): causal + short_taps[:, :, offset, None] * padded[:, :, begin:begin + tokens]  4.31 us
  transfers between devices with their start and end apart: 3, of which 1 were waited for; matrix products, arithmetic and copies ran while one was open for 16% of the time, Pallas kernels for 0%

profile of v1, /device:TPU:0, one launch (start us, length us, event | category | flops | bytes accessed | tf_op | source)
XLA Modules:
  0.0 96.8 jit_solution(13929710109463091467)
XLA Ops:
  0.0 1.3 %pad_maximum_fusion.2 = bf16[3,960,128]{2,1,0:T(8,128)(2,1)S(1)} fusion(bf16[1,960,128]{2,1,0:T(8,128)(2,1)} %bitcast.246, bf16[1,960,128]{2,1,0:T(8,128)(2,1)} %bitcast.250, bf16[1,960,128]{2,1,0:T(8,128)(2,1)} %bitcast.254), kind=kLoop, calls=%fused_computation.55 | loop fusion | flops 737280 | bytes 1474560 | tf_op jit(solution)/shard_map/stack | solution.py:87
  1.9 1.3 %collective-permute-start.1 = (bf16[3,960,6]{1,2,0:T(8,128)(2,1)S(1)}, bf16[3,960,6]{1,2,0:T(8,128)(2,1)S(1)}, u32[]{:S(2)}, u32[]{:S(2)}) collective-permute-start(bf16[3,960,6]{1,2,0:T(8,128)(2,1)S(1)} %copy.29), channel_id=1, source_target_pairs={{1,0},{2,1},{3,2},{4,3},{5,4},{6,5},{7,6},{8,7},{9,8},{10,9},{11,1... | collective-permute-start | bytes 103688 | tf_op jit(solution)/shard_map/ppermute | solution.py:26
  3.5 3.0 %collective-permute-start = (bf16[3,960,6]{1,2,0:T(8,128)(2,1)S(1)}, bf16[3,960,6]{1,2,0:T(8,128)(2,1)S(1)}, u32[]{:S(2)}, u32[]{:S(2)}) collective-permute-start(bf16[3,960,6]{1,2,0:T(8,128)(2,1)S(1)} %copy.25), channel_id=1, source_target_pairs={{0,1},{1,2},{2,3},{3,4},{4,5},{5,6},{6,7},{7,8},{8,9},{9,10},{10,1... | collective-permute-start | bytes 103688 | tf_op jit(solution)/shard_map/ppermute | solution.py:25
  7.3 0.7 reverse.8
  8.1 0.7 reverse.7
  9.0 0.7 reverse.12
  10.4 0.7 reverse.11
  11.2 0.7 reverse.10
  12.7 0.7 reverse.9
  14.1 0.6 copy_bitcast_fusion.20
  15.4 0.7 fusion.60
  16.7 0.7 reverse.13
  18.7 1.2 %copy.30 = bf16[3,960,6]{2,1,0:T(8,128)(2,1)} copy(bf16[3,960,6]{1,2,0:T(8,128)(2,1)S(1)} %collective-permute-done.1) | data formatting | bytes 69120 | tf_op jit(solution)/shard_map/ppermute | solution.py:26
  19.9 2.5 %maximum_maximum_fusion = (bf16[3,960,134]{2,1,0:T(8,128)(2,1)S(1)}, bf16[3,960,134]{2,1,0:T(8,128)(2,1)S(1)}) fusion(bf16[1,960,128]{2,1,0:T(8,128)(2,1)S(1)} %bitcast.247, bf16[1,960,128]{2,1,0:T(8,128)(2,1)S(1)} %bitcast.251, bf16[1,960,128]{2,1,0:T(8,128)(2,1)S(1)} %bitcast.255, bf16[3,960,6]{2,1,0:T(8,128)(2,1)S(1)} %copy.26, bf16[3,960,6]{2,1,0:T(8,128)(2,1)} %copy.30), kind=kLoop, calls=%fused_computation.39 | loop fusion | flops 6174720 | bytes 2350080 | tf_op jit(solution)/shard_map/concatenate | solution.py:27
  22.6 4.5 %fusion.31 = f32[3,960,128]{2,1,0:T(8,128)S(1)} fusion(bf16[3,960,134]{2,1,0:T(8,128)(2,1)S(1)} %get-tuple-element.16, f32[3,960]{1,0:T(4,128)S(1)} %copy-done.13, f32[3,960]{1,0:T(4,128)S(1)} %copy-done.14, f32[3,960]{1,0:T(4,128)S(1)} %copy-done.17, f32[3,960]{1,0:T(4,128)S(1)} %copy-done.18, f32[3,960]{1,0:T(4,128)S(1)} %copy-done.15, ...), kind=kLoop, calls=%fused_computation.38 | loop fusion | flops 8110080 | bytes 6716160 | tf_op jit(solution)/shard_map/add | solution.py:97
  27.1 1.1 %copy-done = f32[3,960,128]{2,1,0:T(8,128)} copy-done((f32[3,960,128]{2,1,0:T(8,128)}, f32[3,960,128]{2,1,0:T(8,128)S(1)}, u32[]{:S(2)}) %copy-start) | copy-done | bytes 1474584
  29.0 4.3 %fusion.25 = f32[3,960,128]{2,1,0:T(8,128)S(1)} fusion(bf16[3,960,134]{2,1,0:T(8,128)(2,1)S(1)} %get-tuple-element.15, f32[3,960]{1,0:T(4,128)S(1)} %get-tuple-element.50, f32[3,960]{1,0:T(4,128)S(1)} %get-tuple-element.51, f32[3,960]{1,0:T(4,128)S(1)} %copy-done.11, f32[3,960]{1,0:T(4,128)S(1)} %copy-done.12, f32[3,960]{1,0:T(4,128)S(1)} %copy-done.9, ...), kind=kLoop, calls=%fused_computation.32 | loop fusion | flops 8110080 | bytes 6716160 | tf_op jit(solution)/shard_map/add | solution.py:94
  33.3 1.1 %copy-done.1 = f32[3,960,128]{2,1,0:T(8,128)} copy-done((f32[3,960,128]{2,1,0:T(8,128)}, f32[3,960,128]{2,1,0:T(8,128)S(1)}, u32[]{:S(2)}) %copy-start.1) | copy-done | bytes 1474584
  34.5 1.3 %copy.31 = bf16[2,960,128]{2,0,1:T(2,128)(2,1)} copy(bf16[2,960,128]{2,1,0:T(8,128)(2,1)S(1)} %pad_maximum_fusion.3) | data formatting | bytes 983040 | tf_op jit(solution)/shard_map/stack | solution.py:102
  35.8 8.1 %all-to-all-start = ((bf16[2,960,128]{2,0,1:T(2,128)(2,1)}), bf16[2,960,128]{2,0,1:T(2,128)(2,1)S(1)}, u32[]{:S(2)}, u32[]{:S(2)}) async-start(bf16[2,960,128]{2,0,1:T(2,128)(2,1)} %copy.31), calls=%async_computation | async-start | bytes 983040 | tf_op jit(solution)/shard_map/all_to_all | solution.py:103
  44.0 0.7 convolution_bitcast_fusion.1
  45.2 2.0 %fusion.17 = f32[60,2,32,128]{3,0,2,1:T(8,128)S(1)} fusion(f32[60,2,32,128]{3,2,0,1:T(8,128)S(1)} %pad_maximum_fusion, f32[1,2,128,128]{3,2,0,1:T(8,128)S(1)} %get-tuple-element.38, f32[1,2,128,128]{3,2,0,1:T(8,128)S(1)} %get-tuple-element.48), kind=kOutput, calls=%fused_computation.25 | convolution fusion | flops 755040256 | bytes 4194304 | tf_op jit(solution)/shard_map/...cfb,cdbk->...dfk/dot_general | solution.py:64
  47.2 10.4 %all-to-all-done = bf16[2,960,128]{2,0,1:T(2,128)(2,1)S(1)} async-done(((bf16[2,960,128]{2,0,1:T(2,128)(2,1)}), bf16[2,960,128]{2,0,1:T(2,128)(2,1)S(1)}, u32[]{:S(2)}, u32[]{:S(2)}) %all-to-all-start) | async-done | bytes 491552 | tf_op jit(solution)/shard_map/all_to_all | solution.py:103
  57.6 1.2 %convolution_bitcast_fusion = f32[2,60,2,32,128]{4,3,1,0,2:T(8,128)S(1)} fusion(bf16[2,16,60,128]{3,0,2,1:T(2,128)(2,1)S(1)} %bitcast.258, f32[1,16,32]{2,1,0:T(8,128)S(1)} %get-tuple-element.62, f32[1,16,32]{2,1,0:T(8,128)S(1)} %get-tuple-element.63), kind=kOutput, calls=%fused_computation.17 | convolution fusion | flops 94372864 | bytes 4427776 | tf_op jit(solution)/shard_map/...ab,caf->...cfb/dot_general | solution.py:54
  58.8 0.8 multiply_add_fusion.1
  60.0 5.0 %fusion.8 = f32[2,60,2,32,128]{4,1,3,2,0:T(8,128)S(1)} fusion(f32[2,60,2,32,128,1]{4,3,1,0,2,5:T(8,128)S(1)} %maximum_bitcast_fusion.1, f32[1,2,128,128]{3,2,0,1:T(8,128)S(1)} %get-tuple-element.38, f32[1,2,128,128]{3,2,0,1:T(8,128)S(1)} %get-tuple-element.48), kind=kOutput, calls=%fused_computation.10 | convolution fusion | flops 1510014976 | bytes 8126464 | tf_op jit(solution)/shard_map/...cfb,cdbk->...dfk/dot_general | solution.py:64
  65.0 1.0 multiply_subtract_fusion.3
  67.3 4.5 %fusion.14 = f32[2,60,2,32,128]{4,3,1,0,2:T(8,128)S(1)} fusion(f32[2,60,2,32,128,1]{4,1,3,2,0,5:T(8,128)S(1)} %maximum_bitcast_fusion, f32[1,2,128,128]{3,2,1,0:T(8,128)S(1)} %copy-done.7, f32[1,2,128,128]{3,2,1,0:T(8,128)S(1)} %copy-done.6), kind=kOutput, calls=%fused_computation.16 | convolution fusion | flops 1510014976 | bytes 8126464 | tf_op jit(solution)/shard_map/...cfk,cdkb->...dfb/dot_general | solution.py:69
  72.4 1.3 %fusion.41 = bf16[2,60,16,128]{3,2,1,0:T(8,128)(2,1)S(1)} fusion(f32[2,60,1,32,128]{4,3,1,0,2:T(8,128)S(1)} %get-tuple-element.10, f32[2,60,1,32,128]{4,3,1,0,2:T(8,128)S(1)} %get-tuple-element.9, f32[1,16,32]{2,1,0:T(8,128)S(1)} %get-tuple-element.62, f32[1,16,32]{2,1,0:T(8,128)S(1)} %get-tuple-element.63), kind=kOutput, calls=%fused_computation.44 | convolution fusion | flops 95847424 | bytes 4427776 | tf_op jit(solution)/shard_map/...cfb,caf->...ab/dot_general | solution.py:79
  74.8 17.7 %all_to_all.20 = bf16[16,2,60,128]{3,1,2,0:T(2,128)(2,1)S(1)} all-to-all(bf16[16,2,60,128]{3,1,2,0:T(2,128)(2,1)S(1)} %constant_dynamic-update-slice_fusion), channel_id=1, replica_groups=mesh['grp'=2,'ctx'=16] {'ctx'}, dimensions={0} | all-to-all | bytes 983040 | tf_op jit(solution)/shard_map/all_to_all | solution.py:14
  92.5 1.7 %slice_reduce_fusion = (bf16[16,60,128]{2,1,0:T(8,128)(2,1)S(1)}, f32[1,16,60,128]{3,0,2,1:T(1,128)S(1)}) fusion(bf16[2,16,60,128]{3,0,2,1:T(2,128)(2,1)S(1)} %bitcast.245), kind=kLoop, calls=%fused_computation.56 | loop fusion | flops 122880 | bytes 1228800 | tf_op jit(solution)/shard_map/slice | solution.py:119
  94.8 2.0 %fusion.46 = bf16[960,128]{1,0:T(8,128)(2,1)} fusion(f32[3,960,128]{2,1,0:T(8,128)} %copy-done, f32[960,128]{1,0:T(8,128)S(1)} %bitcast.259, f32[3,960,128]{2,1,0:T(8,128)} %copy-done.1, bf16[960,128]{1,0:T(8,128)(2,1)S(1)} %rev.8), kind=kLoop, calls=%fused_computation.60 | loop fusion | flops 614400 | bytes 1966080 | tf_op jit(solution)/shard_map/convert_element_type | solution.py:123
  (97 shorter events, 11.7 us)
Async XLA Ops:
  1.3 5.9 %copy-start.8 = (f32[3,960,7]{1,2,0:T(8,128)S(1)}, f32[3,960,7]{1,2,0:T(8,128)}, u32[]{:S(2)}) copy-start(f32[3,960,7]{1,2,0:T(8,128)} %param.8) | copy-start | bytes 241924
  1.6 16.6 %copy-start.5 = (bf16[60,2048]{1,0:T(8,128)(2,1)S(1)}, bf16[60,2048]{1,0:T(8,128)(2,1)}, u32[]{:S(2)}) copy-start(bf16[60,2048]{1,0:T(8,128)(2,1)} %param.9) | copy-start | bytes 737284
  1.9 16.8 %collective-permute-start.1 = (bf16[3,960,6]{1,2,0:T(8,128)(2,1)S(1)}, bf16[3,960,6]{1,2,0:T(8,128)(2,1)S(1)}, u32[]{:S(2)}, u32[]{:S(2)}) collective-permute-start(bf16[3,960,6]{1,2,0:T(8,128)(2,1)S(1)} %copy.29), channel_id=1, source_target_pairs={{1,0},{2,1},{3,2},{4,3},{5,4},{6,5},{7,6},{8,7},{9,8},{10,9},{11,1... | collective-permute-start | bytes 103688 | tf_op jit(solution)/shard_map/ppermute | solution.py:26
  3.5 14.7 %collective-permute-start = (bf16[3,960,6]{1,2,0:T(8,128)(2,1)S(1)}, bf16[3,960,6]{1,2,0:T(8,128)(2,1)S(1)}, u32[]{:S(2)}, u32[]{:S(2)}) collective-permute-start(bf16[3,960,6]{1,2,0:T(8,128)(2,1)S(1)} %copy.25), channel_id=1, source_target_pairs={{0,1},{1,2},{2,3},{3,4},{4,5},{5,6},{6,7},{7,8},{8,9},{9,10},{10,1... | collective-permute-start | bytes 103688 | tf_op jit(solution)/shard_map/ppermute | solution.py:25
  6.9 13.0 %copy-start.2 = (bf16[960,128]{1,0:T(8,128)(2,1)S(1)}, bf16[960,128]{1,0:T(8,128)(2,1)}, u32[]{:S(2)}) copy-start(bf16[960,128]{1,0:T(8,128)(2,1)} %param.7) | copy-start | bytes 737284
  6.9 13.0 %copy-start.3 = (bf16[960,128]{1,0:T(8,128)(2,1)S(1)}, bf16[960,128]{1,0:T(8,128)(2,1)}, u32[]{:S(2)}) copy-start(bf16[960,128]{1,0:T(8,128)(2,1)} %param.6) | copy-start | bytes 737284
  6.9 13.0 %copy-start.4 = (bf16[960,128]{1,0:T(8,128)(2,1)S(1)}, bf16[960,128]{1,0:T(8,128)(2,1)}, u32[]{:S(2)}) copy-start(bf16[960,128]{1,0:T(8,128)(2,1)} %param.5) | copy-start | bytes 737284
  19.9 2.6 %copy-start.13 = (f32[3,960]{1,0:T(4,128)S(1)}, f32[3,960]{1,0:T(4,128)}, u32[]{:S(2)}) copy-start(f32[3,960]{1,0:T(4,128)} %get-tuple-element.56) | copy-start | bytes 34564
  19.9 2.6 %copy-start.14 = (f32[3,960]{1,0:T(4,128)S(1)}, f32[3,960]{1,0:T(4,128)}, u32[]{:S(2)}) copy-start(f32[3,960]{1,0:T(4,128)} %get-tuple-element.57) | copy-start | bytes 34564
  19.9 2.6 %copy-start.15 = (f32[3,960]{1,0:T(4,128)S(1)}, f32[3,960]{1,0:T(4,128)}, u32[]{:S(2)}) copy-start(f32[3,960]{1,0:T(4,128)} %get-tuple-element.60) | copy-start | bytes 34564
  19.9 2.6 %copy-start.16 = (f32[3,960]{1,0:T(4,128)S(1)}, f32[3,960]{1,0:T(4,128)}, u32[]{:S(2)}) copy-start(f32[3,960]{1,0:T(4,128)} %get-tuple-element.61) | copy-start | bytes 34564
  19.9 2.6 %copy-start.17 = (f32[3,960]{1,0:T(4,128)S(1)}, f32[3,960]{1,0:T(4,128)}, u32[]{:S(2)}) copy-start(f32[3,960]{1,0:T(4,128)} %get-tuple-element.58) | copy-start | bytes 34564
  19.9 2.6 %copy-start.18 = (f32[3,960]{1,0:T(4,128)S(1)}, f32[3,960]{1,0:T(4,128)}, u32[]{:S(2)}) copy-start(f32[3,960]{1,0:T(4,128)} %get-tuple-element.59) | copy-start | bytes 34564
  19.9 2.6 %copy-start.20 = (f32[3,960,1]{1,0,2:T(4,128)S(1)}, f32[3,960,1]{1,0,2:T(4,128)}, u32[]{:S(2)}) copy-start(f32[3,960,1]{1,0,2:T(4,128)} %copy.175) | copy-start | bytes 34564
  22.5 6.4 %copy-start.9 = (f32[3,960]{1,0:T(4,128)S(1)}, f32[3,960]{1,0:T(4,128)}, u32[]{:S(2)}) copy-start(f32[3,960]{1,0:T(4,128)} %get-tuple-element.54) | copy-start | bytes 34564
  22.5 6.4 %copy-start.10 = (f32[3,960]{1,0:T(4,128)S(1)}, f32[3,960]{1,0:T(4,128)}, u32[]{:S(2)}) copy-start(f32[3,960]{1,0:T(4,128)} %get-tuple-element.55) | copy-start | bytes 34564
  22.6 6.4 %copy-start.11 = (f32[3,960]{1,0:T(4,128)S(1)}, f32[3,960]{1,0:T(4,128)}, u32[]{:S(2)}) copy-start(f32[3,960]{1,0:T(4,128)} %get-tuple-element.52) | copy-start | bytes 34564
  22.6 6.4 %copy-start.12 = (f32[3,960]{1,0:T(4,128)S(1)}, f32[3,960]{1,0:T(4,128)}, u32[]{:S(2)}) copy-start(f32[3,960]{1,0:T(4,128)} %get-tuple-element.53) | copy-start | bytes 34564
  22.6 6.4 %copy-start.19 = (f32[3,960,1]{1,0,2:T(4,128)S(1)}, f32[3,960,1]{1,0,2:T(4,128)}, u32[]{:S(2)}) copy-start(f32[3,960,1]{1,0,2:T(4,128)} %copy.176) | copy-start | bytes 34564
  27.1 1.1 %copy-start = (f32[3,960,128]{2,1,0:T(8,128)}, f32[3,960,128]{2,1,0:T(8,128)S(1)}, u32[]{:S(2)}) copy-start(f32[3,960,128]{2,1,0:T(8,128)S(1)} %fusion.31) | copy-start | bytes 4423684
  33.3 1.1 %copy-start.1 = (f32[3,960,128]{2,1,0:T(8,128)}, f32[3,960,128]{2,1,0:T(8,128)S(1)}, u32[]{:S(2)}) copy-start(f32[3,960,128]{2,1,0:T(8,128)S(1)} %fusion.25) | copy-start | bytes 4423684
  35.8 21.7 %all-to-all-start = ((bf16[2,960,128]{2,0,1:T(2,128)(2,1)}), bf16[2,960,128]{2,0,1:T(2,128)(2,1)S(1)}, u32[]{:S(2)}, u32[]{:S(2)}) async-start(bf16[2,960,128]{2,0,1:T(2,128)(2,1)} %copy.31), calls=%async_computation | async-start | bytes 983040 | tf_op jit(solution)/shard_map/all_to_all | solution.py:103
  66.3 0.9 copy-start.6
  66.4 1.0 copy-start.7
